TPU v7x, 128 devices: a whole 4x4x4 slice. The times are simulated.
128 devices in a mesh: region: 128 (over x, y, z, core).
Axes of the slice: x: 4, y: 4, z: 4, core: 2. Of those that a mesh axis runs over, the one named last changes fastest.
Arguments:
- node_feat: bfloat16 [65536, 512], P('region'), may hold values from -6 to 6
- edge_feat: bfloat16 [524288, 512], P('region'), may hold values from -6 to 6
- sender: int32 [524288], P('region'), may hold values from 0 to 2815, as said below
- receiver: int32 [524288], P('region'), may hold values from 0 to 512, as said below
- send_list: int32 [128, 8, 32], P('region'), may hold values from 16 to 511
- edge_w1: bfloat16 [1536, 512], replicated, may hold values from -0.15625 to 0.15625
- edge_b1: float32 [512], replicated, may hold values from -4 to 4
- edge_w2: bfloat16 [512, 512], replicated, may hold values from -0.25 to 0.25
- edge_b2: float32 [512], replicated, may hold values from -4 to 4
- edge_gain: float32 [512], replicated, may hold values from 0.5 to 1.5
- edge_shift: float32 [512], replicated, may hold values from -4 to 4
- node_w1: bfloat16 [1024, 512], replicated, may hold values from -0.1875 to 0.1875
- node_b1: float32 [512], replicated, may hold values from -4 to 4
- node_w2: bfloat16 [512, 512], replicated, may hold values from -0.25 to 0.25
- node_b2: float32 [512], replicated, may hold values from -4 to 4
- node_gain: float32 [512], replicated, may hold values from 0.5 to 1.5
- node_shift: float32 [512], replicated, may hold values from -4 to 4
Outputs:
- edge_out: bfloat16 [524288, 512], P('region')
- node_out: bfloat16 [65536, 512], P('region')
Inputs may be any that keep to these rules, and one draw needn't show every extreme that they name: `sender`: a row of the region's table as built in the first step; every region has slots pointing at row 0 and at the last row. `receiver`: non-decreasing within each region's 4096 slots; the value 512 marks an empty slot, and empty slots stand after the used ones; some region uses all its slots. `send_list`: entry [s, j, k] is a local index on region s of a node that s sends to its j-th neighbour.
All inputs are finite; a program needn't handle non-finite values.
Results may differ from a plain program's by a relative error of at most 0.0043.
Values may be sent and summed in bfloat16 or wider, within the bound.
No kernel may reach another device: no remote copies, remote signals or barrier semaphores. Data moves between devices by JAX's collectives and lax.ppermute only.
A program may use at most 128 MiB of HBM per device.

v0:
```python
import jax
import jax.numpy as jnp
from jax import lax
from jax.sharding import PartitionSpec as P

COARSE_DEV = 16
NEIGHBOUR_STEPS = (1, -1, 7, -7, 8, -8, 9, -9)


def from_behind(block, axis, distance):
    devices = range(lax.axis_size(axis))
    route = [((i - distance) % len(devices), i) for i in devices]
    return lax.ppermute(block, axis, route)


def finish(pre, w_second, b_second, gain, shift):
    hidden = jax.nn.silu(pre).astype(jnp.bfloat16)
    out = jnp.dot(hidden, w_second, preferred_element_type=jnp.float32) + b_second
    mean = jnp.mean(out, axis=-1, keepdims=True)
    var = jnp.mean((out - mean) ** 2, axis=-1, keepdims=True)
    return (out - mean) * lax.rsqrt(var + 1e-05) * gain + shift


def pick_rows(wanted_rows, source, block_size):
    total_rows = wanted_rows.shape[0]
    grouped = wanted_rows.reshape(total_rows // block_size, block_size)
    source_ids = jnp.arange(source.shape[0], dtype=jnp.int32)

    def select(group_rows):
        one_hot = (group_rows[:, None] == source_ids[None, :]).astype(source.dtype)
        return jnp.dot(one_hot, source, preferred_element_type=jnp.float32).astype(source.dtype)

    return lax.map(select, grouped).reshape(total_rows, source.shape[1])


def on_device(
    node_feat,
    edge_feat,
    sender,
    receiver,
    send_list,
    edge_w1,
    edge_b1,
    edge_w2,
    edge_b2,
    edge_gain,
    edge_shift,
    node_w1,
    node_b1,
    node_w2,
    node_b2,
    node_gain,
    node_shift,
):
    width = node_feat.shape[1]
    node_rows = node_feat.shape[0]
    edge_rows = edge_feat.shape[0]
    neighbours = send_list.shape[1]
    slots = send_list.shape[2]
    block_size = min(512, edge_rows)
    block_count = edge_rows // block_size
    coarse = node_feat[:COARSE_DEV]
    outgoing = jnp.take(node_feat, send_list[0].reshape(-1), axis=0).reshape(
        neighbours, slots, width
    )
    coarse_all = lax.all_gather(coarse, "region", axis=0, tiled=True)
    arrived = [
        from_behind(rows_out, "region", distance)
        for rows_out, distance in zip(list(outgoing), NEIGHBOUR_STEPS)
    ]
    halo = jnp.concatenate(arrived, axis=0)
    table = jnp.concatenate([node_feat, coarse_all, halo], axis=0)
    live = receiver < node_rows
    recv_index = jnp.minimum(receiver, node_rows - 1)
    sent_rows = pick_rows(sender, table, block_size)
    recv_rows = pick_rows(recv_index, node_feat, block_size)
    inputs = jnp.concatenate([edge_feat, sent_rows, recv_rows], axis=1)
    edge_pre = jnp.dot(inputs, edge_w1, preferred_element_type=jnp.float32) + edge_b1
    update = finish(edge_pre, edge_w2, edge_b2, edge_gain, edge_shift)
    edge_out = jnp.where(live[:, None], edge_feat.astype(jnp.float32) + update, 0.0).astype(
        jnp.bfloat16
    )
    node_ids = jnp.arange(node_rows, dtype=jnp.int32)

    def add_block(position, running):
        first_slot = position * block_size
        block_rows = lax.dynamic_slice_in_dim(edge_out, first_slot, block_size, 0)
        block_ids = lax.dynamic_slice_in_dim(receiver, first_slot, block_size, 0)
        one_hot = (node_ids[:, None] == block_ids[None, :]).astype(jnp.bfloat16)
        return running + jnp.dot(one_hot, block_rows, preferred_element_type=jnp.float32)

    summed = lax.fori_loop(0, block_count, add_block, jnp.zeros((node_rows, width), jnp.float32))
    aggregate = summed.astype(jnp.bfloat16)
    node_in = jnp.concatenate([node_feat, aggregate], axis=1)
    node_pre = jnp.dot(node_in, node_w1, preferred_element_type=jnp.float32) + node_b1
    node_update = finish(node_pre, node_w2, node_b2, node_gain, node_shift)
    node_out = (node_feat.astype(jnp.float32) + node_update).astype(jnp.bfloat16)
    return (edge_out, node_out)


def solution(mesh):
    in_specs = (
        P("region", None),
        P("region", None),
        P("region"),
        P("region"),
        P("region", None, None),
        P(),
        P(),
        P(),
        P(),
        P(),
        P(),
        P(),
        P(),
        P(),
        P(),
        P(),
        P(),
    )
    out_specs = (P("region", None), P("region", None))
    return jax.shard_map(
        on_device, mesh=mesh, in_specs=in_specs, out_specs=out_specs, check_vma=False
    )
```

profile of v0, /device:TPU:0, one launch (start us, length us, event | category | flops | bytes accessed | tf_op | source)
XLA Modules:
  0.0 195.6 jit_solution(12757138436500873263)
XLA Ops:
  7.2 1.4 slice.11
  10.2 2.3 %gather_fusion = bf16[256,512]{1,0:T(8,128)(2,1)S(1)} fusion(bf16[512,512]{1,0:T(8,128)(2,1)} %param.23, s32[1024]{0:T(1024)S(1)} %pad_clamp_fusion), kind=kCustom, calls=%fused_computation | custom fusion | bytes 525312 | tf_op jit(solution)/shard_map/jit(_take)/gather | solution.py:63
  12.8 8.3 %collective-permute-start.1 = (bf16[32,512]{1,0:T(8,128)(2,1)S(1)}, bf16[32,512]{1,0:T(8,128)(2,1)}, u32[]{:S(2)}, u32[]{:S(2)}) collective-permute-start(bf16[32,512]{1,0:T(8,128)(2,1)S(1)} %get-tuple-element.226), channel_id=1, source_target_pairs={{1,0},{2,1},{3,2},{4,3},{5,4},{6,5},{7,6},{8,7},{9,8},{10,9},{11,1... | collective-permute-start | bytes 98312 | tf_op jit(solution)/shard_map/ppermute | solution.py:13
  21.1 5.1 %collective-permute-start.3 = (bf16[32,512]{1,0:T(8,128)(2,1)S(1)}, bf16[32,512]{1,0:T(8,128)(2,1)S(1)}, u32[]{:S(2)}, u32[]{:S(2)}) collective-permute-start(bf16[32,512]{1,0:T(8,128)(2,1)S(1)} %get-tuple-element.224), channel_id=1, source_target_pairs={{7,0},{8,1},{9,2},{10,3},{11,4},{12,5},{13,6},{14,7},{15,8},{16,9}... | collective-permute-start | bytes 98312 | tf_op jit(solution)/shard_map/ppermute | solution.py:13
  26.2 2.0 %copy.20 = bf16[512,512]{0,1:T(8,128)(2,1)} copy(bf16[512,512]{1,0:T(8,128)(2,1)} %param.23) | data formatting | bytes 1048576 | tf_op args[0]
  28.3 6.4 %copy.19 = bf16[4096,512]{0,1:T(8,128)(2,1)} copy(bf16[4096,512]{1,0:T(8,128)(2,1)} %param.24) | data formatting | bytes 8388608 | tf_op args[1]
  35.5 2.3 %broadcast.84.clone = bf16[8,512,512]{2,1,0:T(8,128)(2,1)} broadcast(bf16[]{:T(256)} %constant.76.clone.1), dimensions={} | broadcast | bytes 4194306 | tf_op jit(solution)/shard_map/broadcast.9
  37.8 10.4 %while.37 = (s32[]{:T(128)}, bf16[8,512,512]{2,1,0:T(8,128)(2,1)}, s32[8,512]{1,0:T(8,128)S(1)}, bf16[512,512]{1,0:T(8,128)(2,1)S(1)}, s32[]{:T(128)}) while((s32[]{:T(128)}, bf16[8,512,512]{2,1,0:T(8,128)(2,1)}, s32[8,512]{1,0:T(8,128)S(1)}, bf16[512,512]{1,0:T(8,128)(2,1)S(1)}, s32[]{:T(128)}) %tuple.90), condition=%wide.region_3.4_spmd.clone, body=%wide.region_2.3_spmd.clone.sunk | while | flops 268959744 | bytes 1055297 | solution.py:33
  37.8 1.3 fusion.65
  39.2 1.3 fusion.65
  40.5 1.3 fusion.65
  41.8 1.3 fusion.65
  43.1 1.3 fusion.65
  44.4 1.3 fusion.65
  45.7 1.3 fusion.65
  47.0 1.3 fusion.65
  48.3 30.9 %all-gather.2.cloned.1.call-done = bf16[2048,512]{1,0:T(8,128)(2,1)} async-done(((bf16[16,512]{1,0:T(8,128)(2,1)}), bf16[2048,512]{1,0:T(8,128)(2,1)}) %all-gather.2.cloned.1.call-update) | async-done | bytes 2097168 | tf_op jit(solution)/shard_map/all_gather | solution.py:66
  79.1 3.1 %constant_dynamic-update-slice_fusion.8 = bf16[2816,512]{1,0:T(8,128)(2,1)} fusion(bf16[2816,512]{1,0:T(8,128)(2,1)} %constant_dynamic-update-slice_fusion.9, bf16[2048,512]{1,0:T(8,128)(2,1)} %all-gather.2.cloned.1.call-done), kind=kLoop, calls=%fused_computation.54 | loop fusion | bytes 4194304
  82.2 2.7 %collective-permute-start.5 = (bf16[32,512]{1,0:T(8,128)(2,1)S(1)}, bf16[32,512]{1,0:T(8,128)(2,1)S(1)}, u32[]{:S(2)}, u32[]{:S(2)}) collective-permute-start(bf16[32,512]{1,0:T(8,128)(2,1)S(1)} %get-tuple-element.222), channel_id=1, source_target_pairs={{8,0},{9,1},{10,2},{11,3},{12,4},{13,5},{14,6},{15,7},{16,8},{17,9... | collective-permute-start | bytes 98312 | tf_op jit(solution)/shard_map/ppermute | solution.py:13
  84.9 1.4 constant_dynamic-update-slice_fusion.7
  86.3 1.4 constant_dynamic-update-slice_fusion.6
  87.6 7.5 %collective-permute-start.7 = (bf16[32,512]{1,0:T(8,128)(2,1)S(1)}, bf16[32,512]{1,0:T(8,128)(2,1)S(1)}, u32[]{:S(2)}, u32[]{:S(2)}) collective-permute-start(bf16[32,512]{1,0:T(8,128)(2,1)S(1)} %get-tuple-element.220), channel_id=1, source_target_pairs={{9,0},{10,1},{11,2},{12,3},{13,4},{14,5},{15,6},{16,7},{17,8},{18,... | collective-permute-start | bytes 98312 | tf_op jit(solution)/shard_map/ppermute | solution.py:13
  95.1 1.4 constant_dynamic-update-slice_fusion.5
  99.5 2.3 %broadcast.84.clone.1 = bf16[8,512,512]{2,1,0:T(8,128)(2,1)} broadcast(bf16[]{:T(256)} %constant.76.clone.1), dimensions={} | broadcast | bytes 4194306 | tf_op jit(solution)/shard_map/broadcast.9
  101.8 34.7 %while.36 = (s32[]{:T(128)}, bf16[8,512,512]{2,1,0:T(8,128)(2,1)}, s32[8,512]{1,0:T(8,128)S(1)}, bf16[2816,512]{1,0:T(8,128)(2,1)}, s32[]{:T(128)}) while((s32[]{:T(128)}, bf16[8,512,512]{2,1,0:T(8,128)(2,1)}, s32[8,512]{1,0:T(8,128)S(1)}, bf16[2816,512]{1,0:T(8,128)(2,1)}, s32[]{:T(128)}) %tuple.82), condition=%wide.region_1.2_spmd.clone, body=%wide.region_0.1_spmd.clone.sunk | while | flops 1478098944 | bytes 3414593 | solution.py:33
  101.8 4.4 %fusion.63 = bf16[8,512,512]{2,1,0:T(8,128)(2,1)} fusion(bf16[8,512,512]{2,1,0:T(8,128)(2,1)} %get-tuple-element.328, s32[]{:T(128)} %get-tuple-element.327, bf16[2816,512]{1,0:T(8,128)(2,1)} %get-tuple-element.335, s32[512]{0:T(512)S(1)} %bitcast.34), kind=kOutput, calls=%fused_computation.9.clone.1 | convolution fusion | flops 1478098944 | bytes 3410432 | tf_op jit(solution)/shard_map/while/body/eval_jaxpr/dot_general | solution.py:31
  106.2 4.3 %fusion.63 = bf16[8,512,512]{2,1,0:T(8,128)(2,1)} fusion(bf16[8,512,512]{2,1,0:T(8,128)(2,1)} %get-tuple-element.328, s32[]{:T(128)} %get-tuple-element.327, bf16[2816,512]{1,0:T(8,128)(2,1)} %get-tuple-element.335, s32[512]{0:T(512)S(1)} %bitcast.34), kind=kOutput, calls=%fused_computation.9.clone.1 | convolution fusion | flops 1478098944 | bytes 3410432 | tf_op jit(solution)/shard_map/while/body/eval_jaxpr/dot_general | solution.py:31
  110.5 4.3 %fusion.63 = bf16[8,512,512]{2,1,0:T(8,128)(2,1)} fusion(bf16[8,512,512]{2,1,0:T(8,128)(2,1)} %get-tuple-element.328, s32[]{:T(128)} %get-tuple-element.327, bf16[2816,512]{1,0:T(8,128)(2,1)} %get-tuple-element.335, s32[512]{0:T(512)S(1)} %bitcast.34), kind=kOutput, calls=%fused_computation.9.clone.1 | convolution fusion | flops 1478098944 | bytes 3410432 | tf_op jit(solution)/shard_map/while/body/eval_jaxpr/dot_general | solution.py:31
  114.9 4.3 %fusion.63 = bf16[8,512,512]{2,1,0:T(8,128)(2,1)} fusion(bf16[8,512,512]{2,1,0:T(8,128)(2,1)} %get-tuple-element.328, s32[]{:T(128)} %get-tuple-element.327, bf16[2816,512]{1,0:T(8,128)(2,1)} %get-tuple-element.335, s32[512]{0:T(512)S(1)} %bitcast.34), kind=kOutput, calls=%fused_computation.9.clone.1 | convolution fusion | flops 1478098944 | bytes 3410432 | tf_op jit(solution)/shard_map/while/body/eval_jaxpr/dot_general | solution.py:31
  119.2 4.3 %fusion.63 = bf16[8,512,512]{2,1,0:T(8,128)(2,1)} fusion(bf16[8,512,512]{2,1,0:T(8,128)(2,1)} %get-tuple-element.328, s32[]{:T(128)} %get-tuple-element.327, bf16[2816,512]{1,0:T(8,128)(2,1)} %get-tuple-element.335, s32[512]{0:T(512)S(1)} %bitcast.34), kind=kOutput, calls=%fused_computation.9.clone.1 | convolution fusion | flops 1478098944 | bytes 3410432 | tf_op jit(solution)/shard_map/while/body/eval_jaxpr/dot_general | solution.py:31
  123.5 4.3 %fusion.63 = bf16[8,512,512]{2,1,0:T(8,128)(2,1)} fusion(bf16[8,512,512]{2,1,0:T(8,128)(2,1)} %get-tuple-element.328, s32[]{:T(128)} %get-tuple-element.327, bf16[2816,512]{1,0:T(8,128)(2,1)} %get-tuple-element.335, s32[512]{0:T(512)S(1)} %bitcast.34), kind=kOutput, calls=%fused_computation.9.clone.1 | convolution fusion | flops 1478098944 | bytes 3410432 | tf_op jit(solution)/shard_map/while/body/eval_jaxpr/dot_general | solution.py:31
  127.9 4.3 %fusion.63 = bf16[8,512,512]{2,1,0:T(8,128)(2,1)} fusion(bf16[8,512,512]{2,1,0:T(8,128)(2,1)} %get-tuple-element.328, s32[]{:T(128)} %get-tuple-element.327, bf16[2816,512]{1,0:T(8,128)(2,1)} %get-tuple-element.335, s32[512]{0:T(512)S(1)} %bitcast.34), kind=kOutput, calls=%fused_computation.9.clone.1 | convolution fusion | flops 1478098944 | bytes 3410432 | tf_op jit(solution)/shard_map/while/body/eval_jaxpr/dot_general | solution.py:31
  132.2 4.3 %fusion.63 = bf16[8,512,512]{2,1,0:T(8,128)(2,1)} fusion(bf16[8,512,512]{2,1,0:T(8,128)(2,1)} %get-tuple-element.328, s32[]{:T(128)} %get-tuple-element.327, bf16[2816,512]{1,0:T(8,128)(2,1)} %get-tuple-element.335, s32[512]{0:T(512)S(1)} %bitcast.34), kind=kOutput, calls=%fused_computation.9.clone.1 | convolution fusion | flops 1478098944 | bytes 3410432 | tf_op jit(solution)/shard_map/while/body/eval_jaxpr/dot_general | solution.py:31
  136.6 13.9 %add_reduce_fusion = (f32[4096]{0:T(1024)S(1)}, f32[4096,512]{0,1:T(8,128)}) fusion(f32[512]{0:T(512)S(1)} %copy-done.5, bf16[512,512]{1,0:T(8,128)(2,1)} %param.30, bf16[1536,512]{1,0:T(8,128)(2,1)S(1)} %copy-done, bf16[4096,512]{1,0:T(8,128)(2,1)} %bitcast.32, bf16[4096,512]{1,0:T(8,128)(2,1)} %bitcast.31, bf16[4096,512]{1,0:T(8,128)(2,1)} %param.24, ...), kind=kOutput, calls=%fused_computation.31 | convolution fusion | flops 8644456448 | bytes 23089152 | tf_op jit(solution)/shard_map/dot_general | solution.py:18
  150.5 4.9 %multiply_reduce_fusion = f32[4096]{0:T(1024)S(1)} fusion(f32[4096,512]{0,1:T(8,128)} %get-tuple-element.229, f32[4096]{0:T(1024)S(1)} %broadcast_multiply_fusion, f32[512]{0:T(512)S(1)} %copy-done.5), kind=kLoop, calls=%fused_computation.29 | loop fusion | flops 8384512 | bytes 8423424 | tf_op jit(solution)/shard_map/reduce_sum | solution.py:20
  156.3 6.5 %select_convert_fusion = bf16[4096,512]{0,1:T(8,128)(2,1)} fusion(bf16[4096,512]{0,1:T(8,128)(2,1)} %copy.19, f32[4096,512]{0,1:T(8,128)S(1)} %copy-done.1, f32[512]{0:T(512)S(1)} %copy-done.6, f32[512]{0:T(512)S(1)} %copy-done.7, f32[4096]{0:T(1024)S(1)} %add_rsqrt_fusion, f32[4096]{0:T(1024)S(1)} %broadcast_multiply_fusion, f32[512]{0:T(512)S(1)} %copy-done.5, ...), kind=kLoop, calls=%fused_computation.28 | loop fusion | flops 18874368 | bytes 16820224 | tf_op jit(solution)/shard_map/convert_element_type | solution.py:80
  162.8 6.4 %copy.22 = bf16[4096,512]{1,0:T(8,128)(2,1)} copy(bf16[4096,512]{0,1:T(8,128)(2,1)} %select_convert_fusion) | data formatting | bytes 8388608
  169.2 13.3 %while.38 = (s32[]{:T(128)}, f32[512,512]{1,0:T(8,128)S(1)}, s32[4096]{0:T(1024)S(1)}, bf16[4096,512]{1,0:T(8,128)(2,1)}, s32[]{:T(128)}, /*index=5*/s32[]{:T(128)}, s32[]{:T(128)}, s32[]{:T(128)}) while((s32[]{:T(128)}, f32[512,512]{1,0:T(8,128)S(1)}, s32[4096]{0:T(1024)S(1)}, bf16[4096,512]{1,0:T(8,128)(2,1)}, s32[]{:T(128)}, ...), condition=%wide.region_7.8_spmd.clone, body=%wide.region_6.7_spmd.clone.sunk | while | flops 269221888 | bytes 2627733 | solution.py:92
  169.2 1.6 convolution_add_fusion.4
  170.9 1.6 convolution_add_fusion.4
  172.6 1.6 convolution_add_fusion.4
  174.2 1.6 convolution_add_fusion.4
  175.9 1.6 convolution_add_fusion.4
  177.6 1.6 convolution_add_fusion.4
  179.2 1.6 convolution_add_fusion.4
  180.9 1.6 convolution_add_fusion.4
  183.4 2.8 %fusion.48 = (f32[512]{0:T(512)S(1)}, f32[512,512]{0,1:T(8,128)S(1)}) fusion(f32[512]{0:T(512)S(1)} %copy-done.11, bf16[512,512]{1,0:T(8,128)(2,1)} %param.36, bf16[1024,512]{1,0:T(8,128)(2,1)} %param.34, bf16[512,512]{1,0:T(8,128)(2,1)} %convert_element_type.36, bf16[512,512]{1,0:T(8,128)(2,1)S(1)} %get-tuple-element.362, f32[512]{0:T(512)S(1)} %copy-done.12), kind=kOutput, calls=%fused_computation.71 | convolution fusion | flops 809500160 | bytes 3676160 | tf_op jit(solution)/shard_map/dot_general | solution.py:18
  186.4 1.3 add_convert_fusion
  (89 shorter events, 9.5 us)
Async XLA Ops:
  7.2 129.4 %copy-start = (bf16[1536,512]{1,0:T(8,128)(2,1)S(1)}, bf16[1536,512]{1,0:T(8,128)(2,1)}, u32[]{:S(2)}) copy-start(bf16[1536,512]{1,0:T(8,128)(2,1)} %param.28) | copy-start | bytes 4718596
  7.2 21.0 %copy-start.4 = (s32[4096]{0:T(1024)S(1)}, s32[4096]{0:T(1024)}, u32[]{:S(2)}) copy-start(s32[4096]{0:T(1024)} %param.25) | copy-start | bytes 49156
  7.2 21.0 %copy-start.3 = (s32[4096]{0:T(1024)S(1)}, s32[4096]{0:T(1024)}, u32[]{:S(2)}) copy-start(s32[4096]{0:T(1024)} %param.26) | copy-start | bytes 49156
  7.2 71.9 %all-gather.2.cloned.1.call-start = ((), (), s32[]{:S(2)}) async-start(), calls=%async_computation | async-start | bytes 2113536 | tf_op jit(solution)/shard_map/all_gather | solution.py:66
  12.7 69.5 %collective-permute-start = (bf16[32,512]{1,0:T(8,128)(2,1)S(1)}, bf16[32,512]{1,0:T(8,128)(2,1)}, u32[]{:S(2)}, u32[]{:S(2)}) collective-permute-start(bf16[32,512]{1,0:T(8,128)(2,1)S(1)} %get-tuple-element.227), channel_id=1, source_target_pairs={{127,0},{0,1},{1,2},{2,3},{3,4},{4,5},{5,6},{6,7},{7,8},{8,9},{9,1... | collective-permute-start | bytes 98312 | tf_op jit(solution)/shard_map/ppermute | solution.py:13
  12.8 73.5 %collective-permute-start.1 = (bf16[32,512]{1,0:T(8,128)(2,1)S(1)}, bf16[32,512]{1,0:T(8,128)(2,1)}, u32[]{:S(2)}, u32[]{:S(2)}) collective-permute-start(bf16[32,512]{1,0:T(8,128)(2,1)S(1)} %get-tuple-element.226), channel_id=1, source_target_pairs={{1,0},{2,1},{3,2},{4,3},{5,4},{6,5},{7,6},{8,7},{9,8},{10,9},{11,1... | collective-permute-start | bytes 98312 | tf_op jit(solution)/shard_map/ppermute | solution.py:13
  21.1 66.5 %collective-permute-start.2 = (bf16[32,512]{1,0:T(8,128)(2,1)S(1)}, bf16[32,512]{1,0:T(8,128)(2,1)}, u32[]{:S(2)}, u32[]{:S(2)}) collective-permute-start(bf16[32,512]{1,0:T(8,128)(2,1)S(1)} %get-tuple-element.225), channel_id=1, source_target_pairs={{121,0},{122,1},{123,2},{124,3},{125,4},{126,5},{127,6},{0,7},{1,8... | collective-permute-start | bytes 98312 | tf_op jit(solution)/shard_map/ppermute | solution.py:13
  21.1 75.4 %collective-permute-start.3 = (bf16[32,512]{1,0:T(8,128)(2,1)S(1)}, bf16[32,512]{1,0:T(8,128)(2,1)S(1)}, u32[]{:S(2)}, u32[]{:S(2)}) collective-permute-start(bf16[32,512]{1,0:T(8,128)(2,1)S(1)} %get-tuple-element.224), channel_id=1, source_target_pairs={{7,0},{8,1},{9,2},{10,3},{11,4},{12,5},{13,6},{14,7},{15,8},{16,9}... | collective-permute-start | bytes 98312 | tf_op jit(solution)/shard_map/ppermute | solution.py:13
  26.2 70.9 %collective-permute-start.4 = (bf16[32,512]{1,0:T(8,128)(2,1)S(1)}, bf16[32,512]{1,0:T(8,128)(2,1)S(1)}, u32[]{:S(2)}, u32[]{:S(2)}) collective-permute-start(bf16[32,512]{1,0:T(8,128)(2,1)S(1)} %get-tuple-element.223), channel_id=1, source_target_pairs={{120,0},{121,1},{122,2},{123,3},{124,4},{125,5},{126,6},{127,7},{0... | collective-permute-start | bytes 98312 | tf_op jit(solution)/shard_map/ppermute | solution.py:13
  28.3 6.4 %copy-start.2 = (bf16[512,512]{1,0:T(8,128)(2,1)S(1)}, bf16[512,512]{1,0:T(8,128)(2,1)}, u32[]{:S(2)}) copy-start(bf16[512,512]{1,0:T(8,128)(2,1)} %param.23) | copy-start | bytes 1572868
  82.2 15.5 %collective-permute-start.5 = (bf16[32,512]{1,0:T(8,128)(2,1)S(1)}, bf16[32,512]{1,0:T(8,128)(2,1)S(1)}, u32[]{:S(2)}, u32[]{:S(2)}) collective-permute-start(bf16[32,512]{1,0:T(8,128)(2,1)S(1)} %get-tuple-element.222), channel_id=1, source_target_pairs={{8,0},{9,1},{10,2},{11,3},{12,4},{13,5},{14,6},{15,7},{16,8},{17,9... | collective-permute-start | bytes 98312 | tf_op jit(solution)/shard_map/ppermute | solution.py:13
  86.3 12.1 %collective-permute-start.6 = (bf16[32,512]{1,0:T(8,128)(2,1)S(1)}, bf16[32,512]{1,0:T(8,128)(2,1)S(1)}, u32[]{:S(2)}, u32[]{:S(2)}) collective-permute-start(bf16[32,512]{1,0:T(8,128)(2,1)S(1)} %get-tuple-element.221), channel_id=1, source_target_pairs={{119,0},{120,1},{121,2},{122,3},{123,4},{124,5},{125,6},{126,7},{1... | collective-permute-start | bytes 98312 | tf_op jit(solution)/shard_map/ppermute | solution.py:13
  87.6 11.3 %collective-permute-start.7 = (bf16[32,512]{1,0:T(8,128)(2,1)S(1)}, bf16[32,512]{1,0:T(8,128)(2,1)S(1)}, u32[]{:S(2)}, u32[]{:S(2)}) collective-permute-start(bf16[32,512]{1,0:T(8,128)(2,1)S(1)} %get-tuple-element.220), channel_id=1, source_target_pairs={{9,0},{10,1},{11,2},{12,3},{13,4},{14,5},{15,6},{16,7},{17,8},{18,... | collective-permute-start | bytes 98312 | tf_op jit(solution)/shard_map/ppermute | solution.py:13
  101.8 34.7 %copy-start.5 = (f32[512]{0:T(512)S(1)}, f32[512]{0:T(512)}, u32[]{:S(2)}) copy-start(f32[512]{0:T(512)} %param.31) | copy-start | bytes 6148
  101.8 34.7 %copy-start.10 = (f32[512]{0:T(512)S(1)}, f32[512]{0:T(512)}, u32[]{:S(2)}) copy-start(f32[512]{0:T(512)} %param.29) | copy-start | bytes 6148
  150.5 5.8 %copy-start.1 = (f32[4096,512]{0,1:T(8,128)S(1)}, f32[4096,512]{0,1:T(8,128)}, u32[]{:S(2)}) copy-start(f32[4096,512]{0,1:T(8,128)} %get-tuple-element.229) | copy-start | bytes 25165828
  150.5 5.8 %copy-start.6 = (f32[512]{0:T(512)S(1)}, f32[512]{0:T(512)}, u32[]{:S(2)}) copy-start(f32[512]{0:T(512)} %param.33) | copy-start | bytes 6148
  150.5 5.8 %copy-start.7 = (f32[512]{0:T(512)S(1)}, f32[512]{0:T(512)}, u32[]{:S(2)}) copy-start(f32[512]{0:T(512)} %param.32) | copy-start | bytes 6148
  169.2 14.2 %copy-start.11 = (f32[512]{0:T(512)S(1)}, f32[512]{0:T(512)}, u32[]{:S(2)}) copy-start(f32[512]{0:T(512)} %param.37) | copy-start | bytes 6148
  169.2 14.2 %copy-start.12 = (f32[512]{0:T(512)S(1)}, f32[512]{0:T(512)}, u32[]{:S(2)}) copy-start(f32[512]{0:T(512)} %param.35) | copy-start | bytes 6148
  183.4 3.0 %copy-start.8 = (f32[512]{0:T(512)S(1)}, f32[512]{0:T(512)}, u32[]{:S(2)}) copy-start(f32[512]{0:T(512)} %param.39) | copy-start | bytes 6148
  183.4 3.0 %copy-start.9 = (f32[512]{0:T(512)S(1)}, f32[512]{0:T(512)}, u32[]{:S(2)}) copy-start(f32[512]{0:T(512)} %param.38) | copy-start | bytes 6148
Sparse Core Ops, SparseCore 0:
  11.1 67.9 all-gather.1
where the time goes:
time: 197 us; the launch traced here: 196 us
  matrix products  74.3 us (38%)
  local copies, waits for them, and re-layouts  38.4 us (19%)
  waiting for transfers between devices  30.9 us (16%)
  starting transfers between devices  23.6 us (12%)
  between operations  14.2 us (7%)
  other arithmetic  13.9 us (7%)
    dot_general x16, matrix products, select(): jnp.dot(one_hot, source, preferred_element_type=jnp.float32)  45.1 us
    all_gather x1, waiting for transfers between devices, on_device(): coarse_all = lax.all_gather(coarse, 'region', axis=0, tiled=True)  30.9 us
    unnamed x39, local copies, waits for them, and re-layouts  27.2 us
    ppermute x8, starting transfers between devices, from_behind(): return lax.ppermute(block, axis, route)  23.6 us
    dot_general x2, matrix products, finish(): jnp.dot(hidden, w_second, preferred_element_type=jnp.float32) + b_second  16.7 us
    dot_general x8, matrix products, add_block(): jnp.dot(one_hot, block_rows, preferred_element_type=jnp.float32)  12.5 us
    convert_element_type x1, other arithmetic, on_device(): jnp.where(live[:, None], edge_feat.astype(jnp.float32) + update, 0.0)  6.49 us
    reduce_sum x2, other arithmetic, finish(): var = jnp.mean((out - mean) ** 2, axis=-1, keepdims=True)  5.06 us
  transfers between devices with their start and end apart: 9, of which 1 were waited for; matrix products, arithmetic and copies ran while one was open for 18% of the time, Pallas kernels for 0%

commit v1 on v0

--- a/solution.py
+++ b/solution.py
@@ -63,7 +63,9 @@
     outgoing = jnp.take(node_feat, send_list[0].reshape(-1), axis=0).reshape(
         neighbours, slots, width
     )
-    coarse_all = lax.all_gather(coarse, "region", axis=0, tiled=True)
+    coarse_all = jnp.concatenate(
+        lax.all_to_all(jnp.stack([coarse] * lax.axis_size("region")), "region", 0, 0), axis=0
+    )
     arrived = [
         from_behind(rows_out, "region", distance)
         for rows_out, distance in zip(list(outgoing), NEIGHBOUR_STEPS)

time: 197 us -> 167 us (0.85)
  waiting for transfers between devices: 30.9 us -> 0.02 us
  starting transfers between devices: 23.6 us -> 37.9 us
  between operations: 14.2 us -> 0.82 us
    all_gather x1 -> x0, waiting for transfers between devices: 30.9 us -> none  [on_device(): coarse_all = lax.all_gather(coarse, 'region', axis=0, tiled=True)]
    all_to_all x0 -> x1, starting transfers between devices: none -> 12.9 us  [on_device(): lax.all_to_all(jnp.stack([coarse] * lax.axis_size('region')), 'region', 0...]
    another operation x2 -> x3, local copies, waits for them, and re-layouts: 4.61 us -> 6.25 us
  transfers between devices with their start and end apart: 9 -> 9, of which waited for: 1 -> 0; matrix products, arithmetic and copies ran while one was open for 18% -> 20% of each run, Pallas kernels for 0% -> 0%
where the time goes in v1:
time: 167 us; the launch traced here: 165 us
  matrix products  74.2 us (44%)
  local copies, waits for them, and re-layouts  38.3 us (23%)
  starting transfers between devices  37.9 us (23%)
  other arithmetic  13.9 us (8%)
    dot_general x16, matrix products, select(): jnp.dot(one_hot, source, preferred_element_type=jnp.float32)  45 us
    unnamed x39, local copies, waits for them, and re-layouts  26 us
    ppermute x8, starting transfers between devices, from_behind(): return lax.ppermute(block, axis, route)  25 us
    dot_general x2, matrix products, finish(): jnp.dot(hidden, w_second, preferred_element_type=jnp.float32) + b_second  16.6 us
    all_to_all x1, starting transfers between devices, on_device(): lax.all_to_all(jnp.stack([coarse] * lax.axis_size('region')), 'region', 0...  12.9 us
    dot_general x8, matrix products, add_block(): jnp.dot(one_hot, block_rows, preferred_element_type=jnp.float32)  12.5 us
    convert_element_type x1, other arithmetic, on_device(): jnp.where(live[:, None], edge_feat.astype(jnp.float32) + update, 0.0)  6.49 us
    reduce_sum x2, other arithmetic, finish(): var = jnp.mean((out - mean) ** 2, axis=-1, keepdims=True)  5.06 us
  transfers between devices with their start and end apart: 9, of which 0 were waited for; matrix products, arithmetic and copies ran while one was open for 20% of the time, Pallas kernels for 0%

profile of v1, /device:TPU:0, one launch (start us, length us, event | category | flops | bytes accessed | tf_op | source)
XLA Modules:
  0.0 165.3 jit_solution(4054139315689755106)
XLA Ops:
  2.3 2.3 %gather_fusion = bf16[256,512]{1,0:T(8,128)(2,1)S(1)} fusion(bf16[512,512]{1,0:T(8,128)(2,1)} %param.23, s32[1024]{0:T(1024)S(1)} %pad_clamp_fusion), kind=kCustom, calls=%fused_computation | custom fusion | bytes 525312 | tf_op jit(solution)/shard_map/jit(_take)/gather | solution.py:63
  5.6 1.6 stack.2
  7.2 12.9 %all-to-all-start = ((bf16[128,16,512]{2,1,0:T(8,128)(2,1)}), bf16[128,16,512]{2,1,0:T(8,128)(2,1)}, u32[]{:S(2)}, u32[]{:S(2)}) async-start(bf16[128,16,512]{2,1,0:T(8,128)(2,1)} %stack.2), calls=%async_computation | async-start | bytes 4194304 | tf_op jit(solution)/shard_map/all_to_all | solution.py:67
  20.1 7.0 %collective-permute-start.1 = (bf16[32,512]{1,0:T(8,128)(2,1)S(1)}, bf16[32,512]{1,0:T(8,128)(2,1)}, u32[]{:S(2)}, u32[]{:S(2)}) collective-permute-start(bf16[32,512]{1,0:T(8,128)(2,1)S(1)} %get-tuple-element.226), channel_id=1, source_target_pairs={{1,0},{2,1},{3,2},{4,3},{5,4},{6,5},{7,6},{8,7},{9,8},{10,9},{11,1... | collective-permute-start | bytes 98312 | tf_op jit(solution)/shard_map/ppermute | solution.py:13
  27.2 5.1 %collective-permute-start.3 = (bf16[32,512]{1,0:T(8,128)(2,1)S(1)}, bf16[32,512]{1,0:T(8,128)(2,1)S(1)}, u32[]{:S(2)}, u32[]{:S(2)}) collective-permute-start(bf16[32,512]{1,0:T(8,128)(2,1)S(1)} %get-tuple-element.224), channel_id=1, source_target_pairs={{7,0},{8,1},{9,2},{10,3},{11,4},{12,5},{13,6},{14,7},{15,8},{16,9}... | collective-permute-start | bytes 98312 | tf_op jit(solution)/shard_map/ppermute | solution.py:13
  33.1 1.0 copy.20
  34.1 6.3 %copy.19 = bf16[4096,512]{0,1:T(8,128)(2,1)} copy(bf16[4096,512]{1,0:T(8,128)(2,1)} %param.24) | data formatting | bytes 8388608 | tf_op args[1]
  40.4 2.3 %broadcast.86.clone = bf16[8,512,512]{2,1,0:T(8,128)(2,1)} broadcast(bf16[]{:T(256)} %constant.76.clone.1), dimensions={} | broadcast | bytes 4194306 | tf_op jit(solution)/shard_map/broadcast.9
  42.7 10.4 %while.37 = (s32[]{:T(128)}, bf16[8,512,512]{2,1,0:T(8,128)(2,1)}, s32[8,512]{1,0:T(8,128)S(1)}, bf16[512,512]{1,0:T(8,128)(2,1)S(1)}, s32[]{:T(128)}) while((s32[]{:T(128)}, bf16[8,512,512]{2,1,0:T(8,128)(2,1)}, s32[8,512]{1,0:T(8,128)S(1)}, bf16[512,512]{1,0:T(8,128)(2,1)S(1)}, s32[]{:T(128)}) %tuple.88), condition=%wide.region_3.4_spmd.clone, body=%wide.region_2.3_spmd.clone.sunk | while | flops 268959744 | bytes 1055297 | solution.py:33
  42.8 1.3 fusion.65
  44.1 1.3 fusion.65
  45.4 1.3 fusion.65
  46.7 1.3 fusion.65
  48.0 1.3 fusion.65
  49.3 1.3 fusion.65
  50.6 1.3 fusion.65
  51.9 1.3 fusion.65
  53.2 3.1 %constant_dynamic-update-slice_fusion.8 = bf16[2816,512]{1,0:T(8,128)(2,1)} fusion(bf16[2816,512]{1,0:T(8,128)(2,1)} %constant_dynamic-update-slice_fusion.9, bf16[2048,512]{1,0:T(8,128)(2,1)} %bitcast), kind=kLoop, calls=%fused_computation.54 | loop fusion | bytes 4194304
  56.3 5.4 %collective-permute-start.5 = (bf16[32,512]{1,0:T(8,128)(2,1)S(1)}, bf16[32,512]{1,0:T(8,128)(2,1)S(1)}, u32[]{:S(2)}, u32[]{:S(2)}) collective-permute-start(bf16[32,512]{1,0:T(8,128)(2,1)S(1)} %get-tuple-element.222), channel_id=1, source_target_pairs={{8,0},{9,1},{10,2},{11,3},{12,4},{13,5},{14,6},{15,7},{16,8},{17,9... | collective-permute-start | bytes 98312 | tf_op jit(solution)/shard_map/ppermute | solution.py:13
  61.6 1.4 constant_dynamic-update-slice_fusion.7
  63.0 1.4 constant_dynamic-update-slice_fusion.6
  64.3 7.5 %collective-permute-start.7 = (bf16[32,512]{1,0:T(8,128)(2,1)S(1)}, bf16[32,512]{1,0:T(8,128)(2,1)S(1)}, u32[]{:S(2)}, u32[]{:S(2)}) collective-permute-start(bf16[32,512]{1,0:T(8,128)(2,1)S(1)} %get-tuple-element.220), channel_id=1, source_target_pairs={{9,0},{10,1},{11,2},{12,3},{13,4},{14,5},{15,6},{16,7},{17,8},{18,... | collective-permute-start | bytes 98312 | tf_op jit(solution)/shard_map/ppermute | solution.py:13
  71.8 1.4 constant_dynamic-update-slice_fusion.5
  76.2 2.3 %broadcast.86.clone.1 = bf16[8,512,512]{2,1,0:T(8,128)(2,1)} broadcast(bf16[]{:T(256)} %constant.76.clone.1), dimensions={} | broadcast | bytes 4194306 | tf_op jit(solution)/shard_map/broadcast.9
  78.5 34.7 %while.36 = (s32[]{:T(128)}, bf16[8,512,512]{2,1,0:T(8,128)(2,1)}, s32[8,512]{1,0:T(8,128)S(1)}, bf16[2816,512]{1,0:T(8,128)(2,1)}, s32[]{:T(128)}) while((s32[]{:T(128)}, bf16[8,512,512]{2,1,0:T(8,128)(2,1)}, s32[8,512]{1,0:T(8,128)S(1)}, bf16[2816,512]{1,0:T(8,128)(2,1)}, s32[]{:T(128)}) %tuple.82), condition=%wide.region_1.2_spmd.clone, body=%wide.region_0.1_spmd.clone.sunk | while | flops 1478098944 | bytes 3414593 | solution.py:33
  78.5 4.4 %fusion.63 = bf16[8,512,512]{2,1,0:T(8,128)(2,1)} fusion(bf16[8,512,512]{2,1,0:T(8,128)(2,1)} %get-tuple-element.328, s32[]{:T(128)} %get-tuple-element.327, bf16[2816,512]{1,0:T(8,128)(2,1)} %get-tuple-element.335, s32[512]{0:T(512)S(1)} %bitcast.35), kind=kOutput, calls=%fused_computation.9.clone.1 | convolution fusion | flops 1478098944 | bytes 3410432 | tf_op jit(solution)/shard_map/while/body/eval_jaxpr/dot_general | solution.py:31
  82.9 4.3 %fusion.63 = bf16[8,512,512]{2,1,0:T(8,128)(2,1)} fusion(bf16[8,512,512]{2,1,0:T(8,128)(2,1)} %get-tuple-element.328, s32[]{:T(128)} %get-tuple-element.327, bf16[2816,512]{1,0:T(8,128)(2,1)} %get-tuple-element.335, s32[512]{0:T(512)S(1)} %bitcast.35), kind=kOutput, calls=%fused_computation.9.clone.1 | convolution fusion | flops 1478098944 | bytes 3410432 | tf_op jit(solution)/shard_map/while/body/eval_jaxpr/dot_general | solution.py:31
  87.2 4.3 %fusion.63 = bf16[8,512,512]{2,1,0:T(8,128)(2,1)} fusion(bf16[8,512,512]{2,1,0:T(8,128)(2,1)} %get-tuple-element.328, s32[]{:T(128)} %get-tuple-element.327, bf16[2816,512]{1,0:T(8,128)(2,1)} %get-tuple-element.335, s32[512]{0:T(512)S(1)} %bitcast.35), kind=kOutput, calls=%fused_computation.9.clone.1 | convolution fusion | flops 1478098944 | bytes 3410432 | tf_op jit(solution)/shard_map/while/body/eval_jaxpr/dot_general | solution.py:31
  91.5 4.3 %fusion.63 = bf16[8,512,512]{2,1,0:T(8,128)(2,1)} fusion(bf16[8,512,512]{2,1,0:T(8,128)(2,1)} %get-tuple-element.328, s32[]{:T(128)} %get-tuple-element.327, bf16[2816,512]{1,0:T(8,128)(2,1)} %get-tuple-element.335, s32[512]{0:T(512)S(1)} %bitcast.35), kind=kOutput, calls=%fused_computation.9.clone.1 | convolution fusion | flops 1478098944 | bytes 3410432 | tf_op jit(solution)/shard_map/while/body/eval_jaxpr/dot_general | solution.py:31
  95.9 4.3 %fusion.63 = bf16[8,512,512]{2,1,0:T(8,128)(2,1)} fusion(bf16[8,512,512]{2,1,0:T(8,128)(2,1)} %get-tuple-element.328, s32[]{:T(128)} %get-tuple-element.327, bf16[2816,512]{1,0:T(8,128)(2,1)} %get-tuple-element.335, s32[512]{0:T(512)S(1)} %bitcast.35), kind=kOutput, calls=%fused_computation.9.clone.1 | convolution fusion | flops 1478098944 | bytes 3410432 | tf_op jit(solution)/shard_map/while/body/eval_jaxpr/dot_general | solution.py:31
  100.2 4.3 %fusion.63 = bf16[8,512,512]{2,1,0:T(8,128)(2,1)} fusion(bf16[8,512,512]{2,1,0:T(8,128)(2,1)} %get-tuple-element.328, s32[]{:T(128)} %get-tuple-element.327, bf16[2816,512]{1,0:T(8,128)(2,1)} %get-tuple-element.335, s32[512]{0:T(512)S(1)} %bitcast.35), kind=kOutput, calls=%fused_computation.9.clone.1 | convolution fusion | flops 1478098944 | bytes 3410432 | tf_op jit(solution)/shard_map/while/body/eval_jaxpr/dot_general | solution.py:31
  104.5 4.3 %fusion.63 = bf16[8,512,512]{2,1,0:T(8,128)(2,1)} fusion(bf16[8,512,512]{2,1,0:T(8,128)(2,1)} %get-tuple-element.328, s32[]{:T(128)} %get-tuple-element.327, bf16[2816,512]{1,0:T(8,128)(2,1)} %get-tuple-element.335, s32[512]{0:T(512)S(1)} %bitcast.35), kind=kOutput, calls=%fused_computation.9.clone.1 | convolution fusion | flops 1478098944 | bytes 3410432 | tf_op jit(solution)/shard_map/while/body/eval_jaxpr/dot_general | solution.py:31
  108.9 4.3 %fusion.63 = bf16[8,512,512]{2,1,0:T(8,128)(2,1)} fusion(bf16[8,512,512]{2,1,0:T(8,128)(2,1)} %get-tuple-element.328, s32[]{:T(128)} %get-tuple-element.327, bf16[2816,512]{1,0:T(8,128)(2,1)} %get-tuple-element.335, s32[512]{0:T(512)S(1)} %bitcast.35), kind=kOutput, calls=%fused_computation.9.clone.1 | convolution fusion | flops 1478098944 | bytes 3410432 | tf_op jit(solution)/shard_map/while/body/eval_jaxpr/dot_general | solution.py:31
  113.2 13.8 %add_reduce_fusion = (f32[4096]{0:T(1024)S(1)}, f32[4096,512]{0,1:T(8,128)}) fusion(f32[512]{0:T(512)S(1)} %copy-done.5, bf16[512,512]{1,0:T(8,128)(2,1)} %param.30, bf16[1536,512]{1,0:T(8,128)(2,1)S(1)} %copy-done, bf16[4096,512]{1,0:T(8,128)(2,1)} %bitcast.33, bf16[4096,512]{1,0:T(8,128)(2,1)} %bitcast.32, bf16[4096,512]{1,0:T(8,128)(2,1)} %param.24, ...), kind=kOutput, calls=%fused_computation.31 | convolution fusion | flops 8644456448 | bytes 23089152 | tf_op jit(solution)/shard_map/dot_general | solution.py:18
  127.1 4.9 %multiply_reduce_fusion = f32[4096]{0:T(1024)S(1)} fusion(f32[4096,512]{0,1:T(8,128)} %get-tuple-element.229, f32[4096]{0:T(1024)S(1)} %broadcast_multiply_fusion, f32[512]{0:T(512)S(1)} %copy-done.5), kind=kLoop, calls=%fused_computation.29 | loop fusion | flops 8384512 | bytes 8423424 | tf_op jit(solution)/shard_map/reduce_sum | solution.py:20
  132.8 6.5 %select_convert_fusion = bf16[4096,512]{0,1:T(8,128)(2,1)} fusion(bf16[4096,512]{0,1:T(8,128)(2,1)} %copy.19, f32[4096,512]{0,1:T(8,128)S(1)} %copy-done.1, f32[512]{0:T(512)S(1)} %copy-done.6, f32[512]{0:T(512)S(1)} %copy-done.7, f32[4096]{0:T(1024)S(1)} %add_rsqrt_fusion, f32[4096]{0:T(1024)S(1)} %broadcast_multiply_fusion, f32[512]{0:T(512)S(1)} %copy-done.5, ...), kind=kLoop, calls=%fused_computation.28 | loop fusion | flops 18874368 | bytes 16820224 | tf_op jit(solution)/shard_map/convert_element_type | solution.py:82
  139.3 6.4 %copy.22 = bf16[4096,512]{1,0:T(8,128)(2,1)} copy(bf16[4096,512]{0,1:T(8,128)(2,1)} %select_convert_fusion) | data formatting | bytes 8388608
  145.7 13.3 %while.38 = (s32[]{:T(128)}, f32[512,512]{1,0:T(8,128)S(1)}, s32[4096]{0:T(1024)S(1)}, bf16[4096,512]{1,0:T(8,128)(2,1)}, s32[]{:T(128)}, /*index=5*/s32[]{:T(128)}, s32[]{:T(128)}, s32[]{:T(128)}) while((s32[]{:T(128)}, f32[512,512]{1,0:T(8,128)S(1)}, s32[4096]{0:T(1024)S(1)}, bf16[4096,512]{1,0:T(8,128)(2,1)}, s32[]{:T(128)}, ...), condition=%wide.region_7.8_spmd.clone, body=%wide.region_6.7_spmd.clone.sunk | while | flops 269221888 | bytes 2627733 | solution.py:94
  145.8 1.6 convolution_add_fusion.4
  147.5 1.6 convolution_add_fusion.4
  149.2 1.6 convolution_add_fusion.4
  150.8 1.6 convolution_add_fusion.4
  152.5 1.6 convolution_add_fusion.4
  154.2 1.6 convolution_add_fusion.4
  155.8 1.6 convolution_add_fusion.4
  157.5 1.6 convolution_add_fusion.4
  160.0 2.8 %fusion.48 = (f32[512]{0:T(512)S(1)}, f32[512,512]{0,1:T(8,128)S(1)}) fusion(f32[512]{0:T(512)S(1)} %copy-done.11, bf16[512,512]{1,0:T(8,128)(2,1)} %param.36, bf16[1024,512]{1,0:T(8,128)(2,1)} %param.34, bf16[512,512]{1,0:T(8,128)(2,1)} %convert_element_type.36, bf16[512,512]{1,0:T(8,128)(2,1)S(1)} %get-tuple-element.361, f32[512]{0:T(512)S(1)} %copy-done.12), kind=kOutput, calls=%fused_computation.71 | convolution fusion | flops 809500160 | bytes 3676160 | tf_op jit(solution)/shard_map/dot_general | solution.py:18
  163.0 1.3 add_convert_fusion
  (89 shorter events, 10.2 us)
Async XLA Ops:
  0.6 112.6 %copy-start = (bf16[1536,512]{1,0:T(8,128)(2,1)S(1)}, bf16[1536,512]{1,0:T(8,128)(2,1)}, u32[]{:S(2)}) copy-start(bf16[1536,512]{1,0:T(8,128)(2,1)} %param.28) | copy-start | bytes 4718596
  4.6 27.6 %copy-start.2 = (bf16[512,512]{1,0:T(8,128)(2,1)S(1)}, bf16[512,512]{1,0:T(8,128)(2,1)}, u32[]{:S(2)}) copy-start(bf16[512,512]{1,0:T(8,128)(2,1)} %param.23) | copy-start | bytes 1572868
  4.7 28.4 %copy-start.3 = (s32[4096]{0:T(1024)S(1)}, s32[4096]{0:T(1024)}, u32[]{:S(2)}) copy-start(s32[4096]{0:T(1024)} %param.26) | copy-start | bytes 49156
  4.8 51.4 %collective-permute-start = (bf16[32,512]{1,0:T(8,128)(2,1)S(1)}, bf16[32,512]{1,0:T(8,128)(2,1)}, u32[]{:S(2)}, u32[]{:S(2)}) collective-permute-start(bf16[32,512]{1,0:T(8,128)(2,1)S(1)} %get-tuple-element.227), channel_id=1, source_target_pairs={{127,0},{0,1},{1,2},{2,3},{3,4},{4,5},{5,6},{6,7},{7,8},{8,9},{9,1... | collective-permute-start | bytes 98312 | tf_op jit(solution)/shard_map/ppermute | solution.py:13
  5.6 28.5 %copy-start.4 = (s32[4096]{0:T(1024)S(1)}, s32[4096]{0:T(1024)}, u32[]{:S(2)}) copy-start(s32[4096]{0:T(1024)} %param.25) | copy-start | bytes 49156
  7.2 45.9 %all-to-all-start = ((bf16[128,16,512]{2,1,0:T(8,128)(2,1)}), bf16[128,16,512]{2,1,0:T(8,128)(2,1)}, u32[]{:S(2)}, u32[]{:S(2)}) async-start(bf16[128,16,512]{2,1,0:T(8,128)(2,1)} %stack.2), calls=%async_computation | async-start | bytes 4194304 | tf_op jit(solution)/shard_map/all_to_all | solution.py:67
  20.1 42.8 %collective-permute-start.1 = (bf16[32,512]{1,0:T(8,128)(2,1)S(1)}, bf16[32,512]{1,0:T(8,128)(2,1)}, u32[]{:S(2)}, u32[]{:S(2)}) collective-permute-start(bf16[32,512]{1,0:T(8,128)(2,1)S(1)} %get-tuple-element.226), channel_id=1, source_target_pairs={{1,0},{2,1},{3,2},{4,3},{5,4},{6,5},{7,6},{8,7},{9,8},{10,9},{11,1... | collective-permute-start | bytes 98312 | tf_op jit(solution)/shard_map/ppermute | solution.py:13
  27.1 37.2 %collective-permute-start.2 = (bf16[32,512]{1,0:T(8,128)(2,1)S(1)}, bf16[32,512]{1,0:T(8,128)(2,1)}, u32[]{:S(2)}, u32[]{:S(2)}) collective-permute-start(bf16[32,512]{1,0:T(8,128)(2,1)S(1)} %get-tuple-element.225), channel_id=1, source_target_pairs={{121,0},{122,1},{123,2},{124,3},{125,4},{126,5},{127,6},{0,7},{1,8... | collective-permute-start | bytes 98312 | tf_op jit(solution)/shard_map/ppermute | solution.py:13
  27.2 46.0 %collective-permute-start.3 = (bf16[32,512]{1,0:T(8,128)(2,1)S(1)}, bf16[32,512]{1,0:T(8,128)(2,1)S(1)}, u32[]{:S(2)}, u32[]{:S(2)}) collective-permute-start(bf16[32,512]{1,0:T(8,128)(2,1)S(1)} %get-tuple-element.224), channel_id=1, source_target_pairs={{7,0},{8,1},{9,2},{10,3},{11,4},{12,5},{13,6},{14,7},{15,8},{16,9}... | collective-permute-start | bytes 98312 | tf_op jit(solution)/shard_map/ppermute | solution.py:13
  32.2 41.6 %collective-permute-start.4 = (bf16[32,512]{1,0:T(8,128)(2,1)S(1)}, bf16[32,512]{1,0:T(8,128)(2,1)S(1)}, u32[]{:S(2)}, u32[]{:S(2)}) collective-permute-start(bf16[32,512]{1,0:T(8,128)(2,1)S(1)} %get-tuple-element.223), channel_id=1, source_target_pairs={{120,0},{121,1},{122,2},{123,3},{124,4},{125,5},{126,6},{127,7},{0... | collective-permute-start | bytes 98312 | tf_op jit(solution)/shard_map/ppermute | solution.py:13
  56.3 18.1 %collective-permute-start.5 = (bf16[32,512]{1,0:T(8,128)(2,1)S(1)}, bf16[32,512]{1,0:T(8,128)(2,1)S(1)}, u32[]{:S(2)}, u32[]{:S(2)}) collective-permute-start(bf16[32,512]{1,0:T(8,128)(2,1)S(1)} %get-tuple-element.222), channel_id=1, source_target_pairs={{8,0},{9,1},{10,2},{11,3},{12,4},{13,5},{14,6},{15,7},{16,8},{17,9... | collective-permute-start | bytes 98312 | tf_op jit(solution)/shard_map/ppermute | solution.py:13
  63.0 12.0 %collective-permute-start.6 = (bf16[32,512]{1,0:T(8,128)(2,1)S(1)}, bf16[32,512]{1,0:T(8,128)(2,1)S(1)}, u32[]{:S(2)}, u32[]{:S(2)}) collective-permute-start(bf16[32,512]{1,0:T(8,128)(2,1)S(1)} %get-tuple-element.221), channel_id=1, source_target_pairs={{119,0},{120,1},{121,2},{122,3},{123,4},{124,5},{125,6},{126,7},{1... | collective-permute-start | bytes 98312 | tf_op jit(solution)/shard_map/ppermute | solution.py:13
  64.3 11.3 %collective-permute-start.7 = (bf16[32,512]{1,0:T(8,128)(2,1)S(1)}, bf16[32,512]{1,0:T(8,128)(2,1)S(1)}, u32[]{:S(2)}, u32[]{:S(2)}) collective-permute-start(bf16[32,512]{1,0:T(8,128)(2,1)S(1)} %get-tuple-element.220), channel_id=1, source_target_pairs={{9,0},{10,1},{11,2},{12,3},{13,4},{14,5},{15,6},{16,7},{17,8},{18,... | collective-permute-start | bytes 98312 | tf_op jit(solution)/shard_map/ppermute | solution.py:13
  78.5 34.7 %copy-start.5 = (f32[512]{0:T(512)S(1)}, f32[512]{0:T(512)}, u32[]{:S(2)}) copy-start(f32[512]{0:T(512)} %param.31) | copy-start | bytes 6148
  78.5 34.7 %copy-start.10 = (f32[512]{0:T(512)S(1)}, f32[512]{0:T(512)}, u32[]{:S(2)}) copy-start(f32[512]{0:T(512)} %param.29) | copy-start | bytes 6148
  127.1 5.8 %copy-start.1 = (f32[4096,512]{0,1:T(8,128)S(1)}, f32[4096,512]{0,1:T(8,128)}, u32[]{:S(2)}) copy-start(f32[4096,512]{0,1:T(8,128)} %get-tuple-element.229) | copy-start | bytes 25165828
  127.1 5.8 %copy-start.6 = (f32[512]{0:T(512)S(1)}, f32[512]{0:T(512)}, u32[]{:S(2)}) copy-start(f32[512]{0:T(512)} %param.33) | copy-start | bytes 6148
  127.1 5.8 %copy-start.7 = (f32[512]{0:T(512)S(1)}, f32[512]{0:T(512)}, u32[]{:S(2)}) copy-start(f32[512]{0:T(512)} %param.32) | copy-start | bytes 6148
  145.7 14.2 %copy-start.11 = (f32[512]{0:T(512)S(1)}, f32[512]{0:T(512)}, u32[]{:S(2)}) copy-start(f32[512]{0:T(512)} %param.37) | copy-start | bytes 6148
  145.7 14.2 %copy-start.12 = (f32[512]{0:T(512)S(1)}, f32[512]{0:T(512)}, u32[]{:S(2)}) copy-start(f32[512]{0:T(512)} %param.35) | copy-start | bytes 6148
  159.9 3.0 %copy-start.8 = (f32[512]{0:T(512)S(1)}, f32[512]{0:T(512)}, u32[]{:S(2)}) copy-start(f32[512]{0:T(512)} %param.39) | copy-start | bytes 6148
  159.9 3.0 %copy-start.9 = (f32[512]{0:T(512)S(1)}, f32[512]{0:T(512)}, u32[]{:S(2)}) copy-start(f32[512]{0:T(512)} %param.38) | copy-start | bytes 6148
